TPU v7x, 32 devices: a whole 2x2x4 slice. The times are simulated.
32 devices in a mesh: replica: 8 (over z, core), shard: 4 (over y, x).
Axes of the slice: x: 2, y: 2, z: 4, core: 2. Of those that a mesh axis runs over, the one named last changes fastest.
Arguments:
- local_weights: bfloat16 [8, 8192, 512], P('replica', 'shard'), may hold values from -1.3258252 to 1.3258252
- outer_base: bfloat16 [8192, 512], P('shard'), may hold values from -0.0625 to 0.0625
- momentum: bfloat16 [8192, 512], P('shard', 'replica'), may hold values from -0.06591797 to 0.06591797
- error_feedback: bfloat16 [8, 8192, 512], P('replica', 'shard'), may hold values from -0.032958984 to 0.032958984
- q_start: float32 [512, 32], replicated, may hold values from -6 to 6
- tokens: bfloat16 [8, 512, 8192], P('replica', None, 'shard'), may hold values from -6 to 6
Outputs:
- new_base: bfloat16 [8192, 512], P('shard')
- new_momentum: bfloat16 [8192, 512], P('shard', 'replica')
- new_error: bfloat16 [8, 8192, 512], P('replica', 'shard')
- key_rows: bfloat16 [8, 512, 512], P('replica', 'shard')
All inputs are finite; a program needn't handle non-finite values.
Results may differ from a plain program's by a relative error of at most 0.0065.
Values may be sent and summed in bfloat16 or wider, within the bound.
A program may use at most 64 MiB of HBM per device.

v0:
```python
import jax
import jax.numpy as jnp
from jax import lax
from jax.sharding import PartitionSpec as P

outer_mu = 0.9
outer_rate = 0.7


def on_device(local_weights, outer_base, momentum, error_feedback, q_start, tokens):
    highest = lax.Precision.HIGHEST
    replicas = lax.axis_size("replica")
    own_columns = momentum.shape[1]
    full_momentum = lax.all_gather(momentum, "replica", axis=1, tiled=True)
    pseudo = (
        outer_base.astype(jnp.float32)
        - local_weights[0].astype(jnp.float32)
        + error_feedback[0].astype(jnp.float32)
    )
    p_local = jnp.dot(pseudo, q_start, precision=highest)
    p_mean = lax.psum(p_local, "replica") / replicas
    own_gram = jnp.dot(p_mean.T, p_mean, precision=highest)
    gram_sum = lax.psum(own_gram, "shard")
    factor_low = jnp.linalg.cholesky(gram_sum)
    basis = jax.scipy.linalg.solve_triangular(factor_low, p_mean.T, lower=True).T
    q_raw = jnp.dot(pseudo.T, basis, precision=highest)
    q_mean = lax.psum(q_raw, ("replica", "shard")) / replicas
    update = jnp.dot(basis, q_mean.T, precision=highest)
    new_error = (pseudo - update).astype(jnp.bfloat16)[None]
    moment = outer_mu * full_momentum.astype(jnp.float32) + update
    new_base = (outer_base.astype(jnp.float32) - outer_rate * (outer_mu * moment + update)).astype(
        jnp.bfloat16
    )
    first_column = lax.axis_index("replica") * own_columns
    new_momentum = lax.dynamic_slice_in_dim(moment, first_column, own_columns, 1).astype(
        jnp.bfloat16
    )
    own_tokens = tokens[0]
    key_sum = lax.psum_scatter(
        jnp.dot(own_tokens, new_base, preferred_element_type=jnp.float32),
        "shard",
        scatter_dimension=0,
        tiled=True,
    )
    key_rows = key_sum.astype(jnp.bfloat16)[None]
    return (new_base, new_momentum, new_error, key_rows)


def solution(mesh):
    in_specs = (
        P("replica", "shard", None),
        P("shard", None),
        P("shard", "replica"),
        P("replica", "shard", None),
        P(),
        P("replica", None, "shard"),
    )
    out_specs = (
        P("shard", None),
        P("shard", "replica"),
        P("replica", "shard", None),
        P("replica", "shard", None),
    )
    return jax.shard_map(
        on_device, mesh=mesh, in_specs=in_specs, out_specs=out_specs, check_vma=False
    )
```

profile of v0, /device:TPU:0, one launch (start us, length us, event | category | flops | bytes accessed | tf_op | source)
XLA Modules:
  0.0 319.2 jit_solution(3947755793024692435)
XLA Ops:
  7.2 0.0 copy-start
  7.2 0.0 all-reduce.3.cloned.1.call-start
  7.2 4.1 %copy.10 = bf16[2048,512]{0,1:T(8,128)(2,1)} copy(bf16[2048,512]{1,0:T(8,128)(2,1)} %param.7) | data formatting | bytes 4194304 | tf_op args[1]
  11.3 4.0 %copy.11 = bf16[1,2048,512]{1,2,0:T(8,128)(2,1)} copy(bf16[1,2048,512]{2,1,0:T(8,128)(2,1)} %param.6) | data formatting | bytes 4194304 | tf_op args[0]
  15.3 0.0 copy-start.6
  15.3 3.9 %copy.12 = bf16[1,2048,512]{1,2,0:T(8,128)(2,1)} copy(bf16[1,2048,512]{2,1,0:T(8,128)(2,1)} %param.9) | data formatting | bytes 4194304 | tf_op args[3]
  19.2 0.0 copy-done.6
  19.2 6.8 %fusion.10 = f32[2048,32]{0,1:T(8,128)} fusion(f32[512,32]{0,1:T(8,128)S(1)} %copy-done.6, bf16[2048,512]{0,1:T(8,128)(2,1)} %copy.10, bf16[1,2048,512]{1,2,0:T(8,128)(2,1)} %copy.12, bf16[1,2048,512]{1,2,0:T(8,128)(2,1)} %copy.11), kind=kOutput, calls=%fused_computation.11 | convolution fusion | flops 407896064 | bytes 6619136 | tf_op jit(solution)/shard_map/dot_general | solution.py:20
  26.0 0.0 all-reduce.3.cloned.1.call-update
  26.0 0.0 all-reduce.5.cloned.1.call-start
  26.1 58.3 %all-reduce.3.cloned.1.call-done = f32[2048,32]{0,1:T(8,128)} async-done(((f32[2048,32]{0,1:T(8,128)}), f32[2048,32]{0,1:T(8,128)}) %all-reduce.3.cloned.1.call-update) | async-done | bytes 262160 | tf_op jit(solution)/shard_map/psum | solution.py:21
  84.3 1.4 fusion.16
  85.7 16.0 %psum.22 = f32[32,32]{0,1:T(8,128)S(1)} all-reduce(f32[32,32]{0,1:T(8,128)S(1)} %fusion.16), channel_id=1, replica_groups=mesh['replica'=8,'shard'=4] {'shard'}, use_global_device_ids=true, to_apply=%region_1.0 | all-reduce | flops 1024 | bytes 8192 | tf_op jit(solution)/shard_map/psum | solution.py:23
  101.7 0.1 copy.14
  101.8 2.9 cholesky.16
  104.7 0.6 compare_reduce_fusion
  105.4 0.7 fusion.21
  106.0 2.4 custom-call.7
  108.4 1.4 fusion.14
  109.8 6.4 %fusion.8 = f32[512,32]{1,0:T(8,128)} fusion(f32[32,2048]{1,0:T(8,128)S(1)} %fusion.14, bf16[2048,512]{0,1:T(8,128)(2,1)} %copy.10, bf16[1,2048,512]{1,2,0:T(8,128)(2,1)} %copy.12, bf16[1,2048,512]{1,2,0:T(8,128)(2,1)} %copy.11), kind=kOutput, calls=%fused_computation.10 | convolution fusion | flops 407896064 | bytes 6619136 | tf_op jit(solution)/shard_map/dot_general | solution.py:26
  116.2 0.0 all-reduce.5.cloned.1.call-update
  116.3 0.0 all-gather.2.cloned.1.call-start
  116.3 0.7 all-gather.2.cloned.1.call-update
  117.0 0.2 reduce-scatter.2.cloned.1.call-start
  117.2 123.0 %all-reduce.5.cloned.1.call-done = f32[512,32]{1,0:T(8,128)} async-done(((f32[512,32]{1,0:T(8,128)}), f32[512,32]{1,0:T(8,128)}) %all-reduce.5.cloned.1.call-update) | async-done | bytes 65552 | tf_op jit(solution)/shard_map/psum | solution.py:27
  240.2 29.8 %all-gather.2.cloned.1.call-done = bf16[2048,512]{0,1:T(8,128)(2,1)} async-done(((bf16[2048,64]{0,1:T(8,128)(2,1)}), bf16[2048,512]{0,1:T(8,128)(2,1)}) %all-gather.2.cloned.1.call-update) | async-done | bytes 2097168 | tf_op jit(solution)/shard_map/all_gather | solution.py:14
  270.1 0.0 copy-start.1
  270.1 0.0 copy-start.2
  270.1 0.0 copy-start.3
  270.1 0.0 copy-start.4
  270.1 6.3 %multiply_add_fusion = (bf16[2048,512]{0,1:T(8,128)(2,1)}, f32[2048,512]{0,1:T(8,128)S(1)}) fusion(bf16[2048,512]{0,1:T(8,128)(2,1)} %all-gather.2.cloned.1.call-done, f32[32,2048]{1,0:T(8,128)S(1)} %fusion.14, f32[512,32]{1,0:T(8,128)} %all-reduce.5.cloned.1.call-done), kind=kOutput, calls=%fused_computation.5 | convolution fusion | flops 406863872 | bytes 8716288 | tf_op jit(solution)/shard_map/dot_general | solution.py:28
  276.4 0.0 copy-done.1
  276.4 0.0 copy-done.2
  276.4 0.0 copy-done.3
  276.4 0.0 copy-done.4
  276.4 3.5 %fusion.2 = (bf16[1,2048,512]{1,2,0:T(8,128)(2,1)}, bf16[2048,512]{0,1:T(8,128)(2,1)S(1)}) fusion(f32[2048,512]{0,1:T(8,128)S(1)} %get-tuple-element.11, bf16[1,2048,512]{1,2,0:T(8,128)(2,1)S(1)} %copy-done.3, bf16[1,2048,512]{1,2,0:T(8,128)(2,1)S(1)} %copy-done.2, bf16[2048,512]{0,1:T(8,128)(2,1)S(1)} %copy-done.1, bf16[2048,512]{0,1:T(8,128)(2,1)S(1)} %copy-done.4), kind=kLoop, calls=%fused_computation.6 | loop fusion | flops 15728640 | bytes 16777216 | tf_op jit(solution)/shard_map/broadcast_in_dim | solution.py:29
  279.8 0.0 copy-start.5
  279.9 1.3 copy-done.5
  281.2 0.0 copy-done
  281.2 2.3 fusion.5
  283.4 0.0 reduce-scatter.2.cloned.1.call-update
  283.5 3.9 %copy.15 = bf16[2048,512]{1,0:T(8,128)(2,1)} copy(bf16[2048,512]{0,1:T(8,128)(2,1)} %copy-done.5) | data formatting | bytes 4194304
  287.4 4.0 %copy.16 = bf16[1,2048,512]{2,1,0:T(8,128)(2,1)} copy(bf16[1,2048,512]{1,2,0:T(8,128)(2,1)} %get-tuple-element.8) | data formatting | bytes 4194304
  291.3 1.7 dynamic-slice_convert_fusion
  293.0 17.9 %reduce-scatter.2.cloned.1.call-done = f32[128,512]{0,1:T(8,128)} async-done(((f32[512,512]{0,1:T(8,128)}), f32[128,512]{0,1:T(8,128)}) %reduce-scatter.2.cloned.1.call-update) | async-done | bytes 262160 | tf_op jit(solution)/shard_map/reduce_scatter | solution.py:39
  310.9 1.0 convert_bitcast_fusion
  311.9 0.8 copy.17
  (2 shorter events, 0.0 us)
Async XLA Ops:
  7.2 274.0 %copy-start = (bf16[1,512,2048]{2,1,0:T(8,128)(2,1)S(1)}, bf16[1,512,2048]{2,1,0:T(8,128)(2,1)}, u32[]{:S(2)}) copy-start(bf16[1,512,2048]{2,1,0:T(8,128)(2,1)} %param.11) | copy-start | bytes 6291460
  7.2 77.1 %all-reduce.3.cloned.1.call-start = ((), (), s32[]{:S(2)}) async-start(), calls=%async_computation.2 | async-start | bytes 524288 | tf_op jit(solution)/shard_map/psum | solution.py:21
  15.3 3.9 %copy-start.6 = (f32[512,32]{0,1:T(8,128)S(1)}, f32[512,32]{0,1:T(8,128)}, u32[]{:S(2)}) copy-start(f32[512,32]{0,1:T(8,128)} %param.10) | copy-start | bytes 196612
  26.0 214.2 %all-reduce.5.cloned.1.call-start = ((), (), s32[]{:S(2)}) async-start(), calls=%async_computation.3 | async-start | bytes 524288 | tf_op jit(solution)/shard_map/psum | solution.py:27
  116.3 153.8 %all-gather.2.cloned.1.call-start = ((), (), s32[]{:S(2)}) async-start(), calls=%async_computation.1 | async-start | bytes 2359296 | tf_op jit(solution)/shard_map/all_gather | solution.py:14
  117.0 193.9 %reduce-scatter.2.cloned.1.call-start = ((), (), s32[]{:S(2)}) async-start(), calls=%async_computation.4 | async-start | bytes 1310720 | tf_op jit(solution)/shard_map/reduce_scatter | solution.py:39
  270.1 6.3 %copy-start.1 = (bf16[2048,512]{0,1:T(8,128)(2,1)S(1)}, bf16[2048,512]{0,1:T(8,128)(2,1)}, u32[]{:S(2)}) copy-start(bf16[2048,512]{0,1:T(8,128)(2,1)} %copy.10) | copy-start | bytes 6291460
  270.1 6.3 %copy-start.2 = (bf16[1,2048,512]{1,2,0:T(8,128)(2,1)S(1)}, bf16[1,2048,512]{1,2,0:T(8,128)(2,1)}, u32[]{:S(2)}) copy-start(bf16[1,2048,512]{1,2,0:T(8,128)(2,1)} %copy.11) | copy-start | bytes 6291460
  270.1 6.3 %copy-start.3 = (bf16[1,2048,512]{1,2,0:T(8,128)(2,1)S(1)}, bf16[1,2048,512]{1,2,0:T(8,128)(2,1)}, u32[]{:S(2)}) copy-start(bf16[1,2048,512]{1,2,0:T(8,128)(2,1)} %copy.12) | copy-start | bytes 6291460
  270.1 6.3 %copy-start.4 = (bf16[2048,512]{0,1:T(8,128)(2,1)S(1)}, bf16[2048,512]{0,1:T(8,128)(2,1)}, u32[]{:S(2)}) copy-start(bf16[2048,512]{0,1:T(8,128)(2,1)} %all-gather.2.cloned.1.call-done) | copy-start | bytes 6291460
  279.8 1.3 copy-start.5
Sparse Core Ops, SparseCore 0:
  26.1 58.1 all-reduce.2
  116.4 123.7 all-reduce.4
  241.8 28.1 all-gather.1
  283.6 27.3 reduce-scatter.1
where the time goes:
time: 320 us; the launch traced here: 319 us
  waiting for transfers between devices  230 us (72%)
  matrix products  24.5 us (8%)
  local copies, waits for them, and re-layouts  23.7 us (7%)
  blocking collectives  16 us (5%)
  between operations  13.8 us (4%)
  other arithmetic  11.1 us (3%)
    psum x1, waiting for transfers between devices, on_device(): q_mean = lax.psum(q_raw, ('replica', 'shard')) / replicas  123 us
    psum x1, waiting for transfers between devices, on_device(): p_mean = lax.psum(p_local, 'replica') / replicas  58.3 us
    all_gather x1, waiting for transfers between devices, on_device(): full_momentum = lax.all_gather(momentum, 'replica', axis=1, tiled=True)  29.8 us
    unnamed x20, local copies, waits for them, and re-layouts  22 us
    reduce_scatter x1, waiting for transfers between devices, on_device(): lax.psum_scatter(jnp.dot(own_tokens, new_base, preferred_element_type=jnp...  17.9 us
    psum x1, blocking collectives, on_device(): gram_sum = lax.psum(own_gram, 'shard')  16 us
    dot_general x1, matrix products, on_device(): p_local = jnp.dot(pseudo, q_start, precision=highest)  6.77 us
  transfers between devices with their start and end apart: 4, of which 4 were waited for; matrix products, arithmetic and copies ran while one was open for 3% of the time, Pallas kernels for 0%

commit v1 on v0

--- a/solution.py
+++ b/solution.py
@@ -11,7 +11,11 @@
     highest = lax.Precision.HIGHEST
     replicas = lax.axis_size("replica")
     own_columns = momentum.shape[1]
-    full_momentum = lax.all_gather(momentum, "replica", axis=1, tiled=True)
+
+    def body_derive(m, along_axis, in_dim):
+        return jnp.concatenate(lax.all_gather(m, axis_name=along_axis), axis=in_dim)
+
+    full_momentum = body_derive(momentum, "replica", 1)
     pseudo = (
         outer_base.astype(jnp.float32)
         - local_weights[0].astype(jnp.float32)

time: 320 us -> 296 us (0.925)
  waiting for transfers between devices: 230 us -> 201 us
  matrix products: 24.5 us -> 28 us
    all_gather x1, waiting for transfers between devices: 29.8 us -> 0.02 us  [body_derive(): return jnp.concatenate(lax.all_gather(m, axis_name=along_axis), axis=in_dim)]
    dot_general x1, matrix products: 6.28 us -> 9.8 us  [on_device(): update = jnp.dot(basis, q_mean.T, precision=highest)]
    broadcast_in_dim x1 -> x0, other arithmetic: 3.47 us -> none  [on_device(): new_error = (pseudo - update).astype(jnp.bfloat16)[None]]
    unnamed x20 -> x12, local copies, waits for them, and re-layouts: 22 us -> 21.9 us
  transfers between devices with their start and end apart: 4 -> 4, of which waited for: 4 -> 3; matrix products, arithmetic and copies ran while one was open for 3% -> 10% of each run, Pallas kernels for 0% -> 0%
where the time goes in v1:
time: 296 us; the launch traced here: 295 us
  waiting for transfers between devices  201 us (68%)
  matrix products  28 us (9%)
  local copies, waits for them, and re-layouts  25.8 us (9%)
  blocking collectives  16 us (5%)
  between operations  13.8 us (5%)
  other arithmetic  9.59 us (3%)
    psum x1, waiting for transfers between devices, on_device(): q_mean = lax.psum(q_raw, ('replica', 'shard')) / replicas  126 us
    psum x1, waiting for transfers between devices, on_device(): p_mean = lax.psum(p_local, 'replica') / replicas  57.5 us
    unnamed x12, local copies, waits for them, and re-layouts  21.9 us
    reduce_scatter x1, waiting for transfers between devices, on_device(): lax.psum_scatter(jnp.dot(own_tokens, new_base, preferred_element_type=jnp...  17.6 us
    psum x1, blocking collectives, on_device(): gram_sum = lax.psum(own_gram, 'shard')  16 us
    dot_general x1, matrix products, on_device(): update = jnp.dot(basis, q_mean.T, precision=highest)  9.8 us
    dot_general x1, matrix products, on_device(): p_local = jnp.dot(pseudo, q_start, precision=highest)  6.77 us
    dot_general x1, matrix products, on_device(): q_raw = jnp.dot(pseudo.T, basis, precision=highest)  6.43 us
  transfers between devices with their start and end apart: 4, of which 3 were waited for; matrix products, arithmetic and copies ran while one was open for 10% of the time, Pallas kernels for 0%

profile of v1, /device:TPU:0, one launch (start us, length us, event | category | flops | bytes accessed | tf_op | source)
XLA Modules:
  0.0 295.1 jit_solution(2912820521338833623)
XLA Ops:
  7.2 0.0 copy-start
  7.2 0.0 all-reduce.3.cloned.1.call-start
  7.2 4.1 %copy.10 = bf16[2048,512]{0,1:T(8,128)(2,1)} copy(bf16[2048,512]{1,0:T(8,128)(2,1)} %param.7) | data formatting | bytes 4194304 | tf_op args[1]
  11.3 3.9 %copy.13 = bf16[1,2048,512]{1,2,0:T(8,128)(2,1)} copy(bf16[1,2048,512]{2,1,0:T(8,128)(2,1)} %param.9) | data formatting | bytes 4194304 | tf_op args[3]
  15.2 0.0 copy-start.2
  15.2 4.0 %copy.12 = bf16[1,2048,512]{1,2,0:T(8,128)(2,1)} copy(bf16[1,2048,512]{2,1,0:T(8,128)(2,1)} %param.6) | data formatting | bytes 4194304 | tf_op args[0]
  19.2 0.0 copy-done.2
  19.2 6.8 %fusion.10 = f32[2048,32]{0,1:T(8,128)} fusion(f32[512,32]{0,1:T(8,128)S(1)} %copy-done.2, bf16[2048,512]{0,1:T(8,128)(2,1)} %copy.10, bf16[1,2048,512]{1,2,0:T(8,128)(2,1)} %copy.13, bf16[1,2048,512]{1,2,0:T(8,128)(2,1)} %copy.12), kind=kOutput, calls=%fused_computation.13 | convolution fusion | flops 407896064 | bytes 6619136 | tf_op jit(solution)/shard_map/dot_general | solution.py:24
  25.9 0.0 all-reduce.3.cloned.1.call-update
  26.0 0.0 all-gather.3.cloned.1.call-start
  26.0 0.7 all-gather.3.cloned.1.call-update
  26.7 0.0 all-reduce.5.cloned.1.call-start
  26.8 57.5 %all-reduce.3.cloned.1.call-done = f32[2048,32]{0,1:T(8,128)} async-done(((f32[2048,32]{0,1:T(8,128)}), f32[2048,32]{0,1:T(8,128)}) %all-reduce.3.cloned.1.call-update) | async-done | bytes 262160 | tf_op jit(solution)/shard_map/psum | solution.py:25
  84.3 1.4 fusion.16
  85.7 16.0 %psum.22 = f32[32,32]{0,1:T(8,128)S(1)} all-reduce(f32[32,32]{0,1:T(8,128)S(1)} %fusion.16), channel_id=1, replica_groups=mesh['replica'=8,'shard'=4] {'shard'}, use_global_device_ids=true, to_apply=%region_1.0 | all-reduce | flops 1024 | bytes 8192 | tf_op jit(solution)/shard_map/psum | solution.py:27
  101.6 0.1 copy.15
  101.7 2.9 cholesky.16
  104.7 0.6 compare_reduce_fusion
  105.3 0.7 fusion.21
  106.0 2.4 custom-call.7
  108.4 1.4 fusion.14
  109.8 6.4 %fusion.8 = f32[512,32]{1,0:T(8,128)} fusion(f32[32,2048]{1,0:T(8,128)S(1)} %fusion.14, bf16[2048,512]{0,1:T(8,128)(2,1)} %copy.10, bf16[1,2048,512]{1,2,0:T(8,128)(2,1)} %copy.13, bf16[1,2048,512]{1,2,0:T(8,128)(2,1)} %copy.12), kind=kOutput, calls=%fused_computation.12 | convolution fusion | flops 407896064 | bytes 6619136 | tf_op jit(solution)/shard_map/dot_general | solution.py:30
  116.2 0.0 all-reduce.5.cloned.1.call-update
  116.3 0.2 reduce-scatter.2.cloned.1.call-start
  116.5 0.0 all-gather.3.cloned.1.call-done
  116.5 1.9 convert_multiply_fusion
  118.5 2.2 copy.22
  120.7 125.6 %all-reduce.5.cloned.1.call-done = f32[512,32]{1,0:T(8,128)} async-done(((f32[512,32]{1,0:T(8,128)}), f32[512,32]{1,0:T(8,128)}) %all-reduce.5.cloned.1.call-update) | async-done | bytes 65552 | tf_op jit(solution)/shard_map/psum | solution.py:31
  246.2 9.8 %fusion.1 = (bf16[2048,512]{0,1:T(8,128)(2,1)S(1)}, bf16[2048,512]{0,1:T(8,128)(2,1)}, bf16[1,2048,512]{1,2,0:T(8,128)(2,1)}) fusion(bf16[2048,512]{0,1:T(8,128)(2,1)} %copy.10, f32[8,2048,64]{1,2,0:T(8,128)} %bitcast.48, bf16[1,2048,512]{1,2,0:T(8,128)(2,1)} %copy.13, bf16[1,2048,512]{1,2,0:T(8,128)(2,1)} %copy.12, f32[32,2048]{1,0:T(8,128)S(1)} %fusion.14, ...), kind=kOutput, calls=%fused_computation.3 | convolution fusion | flops 417349632 | bytes 17104896 | tf_op jit(solution)/shard_map/dot_general | solution.py:32
  256.0 0.0 copy-start.1
  256.0 1.3 copy-done.1
  257.4 0.0 copy-done
  257.4 2.3 fusion.5
  259.6 0.0 reduce-scatter.2.cloned.1.call-update
  259.7 3.9 %copy.16 = bf16[2048,512]{1,0:T(8,128)(2,1)} copy(bf16[2048,512]{0,1:T(8,128)(2,1)} %copy-done.1) | data formatting | bytes 4194304
  263.6 3.9 %copy.17 = bf16[1,2048,512]{2,1,0:T(8,128)(2,1)} copy(bf16[1,2048,512]{1,2,0:T(8,128)(2,1)} %get-tuple-element.10) | data formatting | bytes 4194304
  267.5 1.7 dynamic-slice_convert_fusion
  269.2 17.6 %reduce-scatter.2.cloned.1.call-done = f32[128,512]{0,1:T(8,128)} async-done(((f32[512,512]{0,1:T(8,128)}), f32[128,512]{0,1:T(8,128)}) %reduce-scatter.2.cloned.1.call-update) | async-done | bytes 262160 | tf_op jit(solution)/shard_map/reduce_scatter | solution.py:43
  286.8 1.0 convert_bitcast_fusion
  287.8 0.8 copy.18
  (2 shorter events, 0.0 us)
Async XLA Ops:
  7.2 250.2 %copy-start = (bf16[1,512,2048]{2,1,0:T(8,128)(2,1)S(1)}, bf16[1,512,2048]{2,1,0:T(8,128)(2,1)}, u32[]{:S(2)}) copy-start(bf16[1,512,2048]{2,1,0:T(8,128)(2,1)} %param.11) | copy-start | bytes 6291460
  7.2 77.1 %all-reduce.3.cloned.1.call-start = ((), (), s32[]{:S(2)}) async-start(), calls=%async_computation.1 | async-start | bytes 524288 | tf_op jit(solution)/shard_map/psum | solution.py:25
  15.2 4.0 %copy-start.2 = (f32[512,32]{0,1:T(8,128)S(1)}, f32[512,32]{0,1:T(8,128)}, u32[]{:S(2)}) copy-start(f32[512,32]{0,1:T(8,128)} %param.10) | copy-start | bytes 196612
  26.0 90.6 %all-gather.3.cloned.1.call-start = ((), (), s32[]{:S(2)}) async-start(), calls=%async_computation.4 | async-start | bytes 2359296 | tf_op jit(solution)/shard_map/all_gather | solution.py:16
  26.7 219.5 %all-reduce.5.cloned.1.call-start = ((), (), s32[]{:S(2)}) async-start(), calls=%async_computation.2 | async-start | bytes 524288 | tf_op jit(solution)/shard_map/psum | solution.py:31
  116.3 170.5 %reduce-scatter.2.cloned.1.call-start = ((), (), s32[]{:S(2)}) async-start(), calls=%async_computation.3 | async-start | bytes 1310720 | tf_op jit(solution)/shard_map/reduce_scatter | solution.py:43
  256.0 1.3 copy-start.1
Sparse Core Ops, SparseCore 0:
  26.1 58.1 all-reduce.2
  85.9 28.1 all-gather.2
  120.2 126.0 all-reduce.4
  259.8 26.9 reduce-scatter.1
